TPU v7x, 32 devices: a whole 2x2x4 slice. The times are simulated.
32 devices in a mesh: dp: 4 (over y, x), ep: 8 (over z, core).
Axes of the slice: x: 2, y: 2, z: 4, core: 2. Of those that a mesh axis runs over, the one named last changes fastest.
Arguments:
- attn_heads: bfloat16 [8, 256, 2048], P('ep', None, 'dp'), may hold values from -6 to 6
- residual: bfloat16 [8, 256, 2048], P('ep', 'dp'), may hold values from -6 to 6
- w_out: bfloat16 [2048, 2048], P('dp'), may hold values from -0.125 to 0.125
- gain_post: bfloat16 [2048], replicated, may hold values from 0.5 to 1.5
- w_router: bfloat16 [2048, 60], replicated, may hold values from -0.125 to 0.125
- expert_ids: int32 [8, 256, 4], P('ep', 'dp'), may hold values from 0 to 59, all different within a row; in each aligned block of 64 rows (0 to 63, 64 to 127, ..., all dimensions but the last counted through in order) at most 8 rows name the same one
- expert_slot: int32 [60], replicated, may hold values from 0 to 63, as said below
- w_gate: bfloat16 [64, 2048, 1408], P('ep', None, 'dp'), may hold values from -0.125 to 0.125
- w_up: bfloat16 [64, 2048, 1408], P('ep', None, 'dp'), may hold values from -0.125 to 0.125
- w_down: bfloat16 [64, 1408, 2048], P('ep', 'dp'), may hold values from -0.15625 to 0.15625
- w_shared_gate: bfloat16 [2048, 5632], P(None, 'ep'), may hold values from -0.125 to 0.125
- w_shared_up: bfloat16 [2048, 5632], P(None, 'ep'), may hold values from -0.125 to 0.125
- w_shared_down: bfloat16 [5632, 2048], P('ep'), may hold values from -0.078125 to 0.078125
- w_shared_score: bfloat16 [2048], replicated, may hold values from -0.125 to 0.125
- gain_final: bfloat16 [2048], replicated, may hold values from 0.5 to 1.5
Outputs:
- mixed_out: bfloat16 [8, 256, 2048], P('ep', 'dp')
- final_out: bfloat16 [8, 256, 2048], P('ep', 'dp')
Inputs may be any that keep to these rules, and one draw needn't show every extreme that they name: `expert_ids`: each row names 4 different experts. Within the 64 rows of one device no expert is named by more than 8 rows, and in some device one expert is named by exactly 8 rows. All entries differ; expert e uses entry expert_slot[e] of w_gate, w_up and w_down, and index i of ep holds positions i * 8 to (i + 1) * 8 - 1.
All inputs are finite; a program needn't handle non-finite values.
Results may differ from a plain program's by a relative error of at most 0.02.
Values may be sent and summed in bfloat16 or wider, within the bound.
A program may use at most 128 MiB of HBM per device.

v0:
```python
import jax
import jax.numpy as jnp
from jax import lax
from jax.sharding import PartitionSpec as P

MOST = 8
eps_norm = 1e-06


def rms_scale(values_in, gain_vec):
    values = values_in.astype(jnp.float32)
    return (
        values
        * lax.rsqrt(jnp.mean(values * values, axis=-1, keepdims=True) + eps_norm)
        * gain_vec.astype(jnp.float32)
    )


def expert_partial(rows_in, w_gate, w_up, w_down):
    gate_part = jnp.einsum("semd,edf->semf", rows_in, w_gate, preferred_element_type=jnp.float32)
    up_part = jnp.einsum("semd,edf->semf", rows_in, w_up, preferred_element_type=jnp.float32)
    hidden = (jax.nn.silu(gate_part) * up_part).astype(jnp.bfloat16)
    return jnp.einsum("semf,efd->semd", hidden, w_down, preferred_element_type=jnp.float32)


def per_device(
    attn_heads,
    residual,
    w_out,
    gain_post,
    w_router,
    expert_ids,
    expert_slot,
    w_gate,
    w_up,
    w_down,
    w_shared_gate,
    w_shared_up,
    w_shared_down,
    w_shared_score,
    gain_final,
):
    local_heads = attn_heads[0]
    model_width = residual.shape[2]
    row_block = local_heads
    projected = lax.psum_scatter(
        jnp.dot(row_block, w_out, preferred_element_type=jnp.float32).astype(jnp.bfloat16),
        "dp",
        scatter_dimension=0,
        tiled=True,
    ).astype(jnp.float32)
    hidden_state = (residual[0].astype(jnp.float32) + projected).astype(jnp.bfloat16)
    normed = rms_scale(hidden_state, gain_post).astype(jnp.bfloat16)
    logits = jnp.dot(normed, w_router, preferred_element_type=jnp.float32)
    chosen = expert_ids[0]
    expert_count = w_router.shape[1]
    one_hot = chosen[:, :, None] == jnp.arange(expert_count, dtype=jnp.int32)[None, None, :]
    picked = jnp.sum(jnp.where(one_hot, logits[:, None, :], 0.0), axis=2)
    exp_logits = jnp.exp(picked)
    route_weights = (exp_logits / jnp.sum(exp_logits, axis=1, keepdims=True)).astype(jnp.bfloat16)
    experts_here = w_gate.shape[0]
    groups = lax.axis_size("ep")
    positions = experts_here * groups
    buffer_cells = positions * MOST
    expert_hits = jnp.any(one_hot, axis=1).astype(jnp.int32)
    earlier = jnp.cumsum(expert_hits, axis=0) - expert_hits
    slot_rank = jnp.sum(jnp.where(one_hot, earlier[:, None, :], 0), axis=2)
    position = jnp.sum(jnp.where(one_hot, expert_slot[None, None, :], 0), axis=2)
    buffer_index = position * MOST + slot_rank
    placed = buffer_index[:, :, None] == jnp.arange(buffer_cells, dtype=jnp.int32)[None, None, :]
    dispatch_mat = jnp.any(placed, axis=1).astype(jnp.bfloat16)
    combine_mat = jnp.sum(
        jnp.where(placed, route_weights.astype(jnp.float32)[:, :, None], 0.0), axis=1
    ).astype(jnp.bfloat16)
    outgoing = jnp.einsum(
        "rc,rd->cd", dispatch_mat, normed, preferred_element_type=jnp.float32
    ).astype(jnp.bfloat16)
    outgoing = outgoing.reshape(groups, experts_here, MOST, model_width)
    dp_count = lax.axis_size("dp")
    copies = jnp.broadcast_to(outgoing[None], (dp_count,) + outgoing.shape).reshape(
        (dp_count * groups, experts_here, MOST, model_width)
    )
    partial_value = expert_partial(
        lax.all_to_all(copies, ("dp", "ep"), split_axis=0, concat_axis=0, tiled=True),
        w_gate,
        w_up,
        w_down,
    ).astype(jnp.bfloat16)
    returned_all = lax.all_to_all(
        partial_value, ("dp", "ep"), split_axis=0, concat_axis=0, tiled=True
    )
    returned = jnp.sum(
        returned_all.reshape(dp_count, groups, experts_here, MOST, model_width).astype(jnp.float32),
        axis=0,
    ).astype(jnp.bfloat16)
    routed = jnp.dot(
        combine_mat, returned.reshape(buffer_cells, model_width), preferred_element_type=jnp.float32
    )
    row_block = lax.all_gather(normed, "ep", axis=0, tiled=True)
    gate_part = jnp.dot(row_block, w_shared_gate, preferred_element_type=jnp.float32)
    up_part = jnp.dot(row_block, w_shared_up, preferred_element_type=jnp.float32)
    hidden_all = (jax.nn.silu(gate_part) * up_part).astype(jnp.bfloat16)
    row_block = hidden_all
    shared_sum = lax.psum_scatter(
        jnp.dot(row_block, w_shared_down, preferred_element_type=jnp.float32).astype(jnp.bfloat16),
        "ep",
        scatter_dimension=0,
        tiled=True,
    ).astype(jnp.float32)
    shared_score = jax.nn.sigmoid(
        jnp.dot(normed, w_shared_score, preferred_element_type=jnp.float32)
    )
    mixed_out = (
        hidden_state.astype(jnp.float32) + shared_score[:, None] * shared_sum + routed
    ).astype(jnp.bfloat16)
    final_out = rms_scale(mixed_out, gain_final).astype(jnp.bfloat16)
    return (mixed_out[None], final_out[None])


def solution(mesh):
    in_specs = (
        P("ep", None, "dp"),
        P("ep", "dp", None),
        P("dp", None),
        P(),
        P(),
        P("ep", "dp", None),
        P(),
        P("ep", None, "dp"),
        P("ep", None, "dp"),
        P("ep", "dp", None),
        P(None, "ep"),
        P(None, "ep"),
        P("ep", None),
        P(),
        P(),
    )
    out_specs = (P("ep", "dp", None), P("ep", "dp", None))
    return jax.shard_map(
        per_device, mesh=mesh, in_specs=in_specs, out_specs=out_specs, check_vma=False
    )
```

profile of v0, /device:TPU:0, one launch (start us, length us, event | category | flops | bytes accessed | tf_op | source)
XLA Modules:
  0.0 522.7 jit_solution(2066058382093305351)
XLA Ops:
  7.3 3.5 convolution_convert_fusion.2
  11.3 0.1 select_reduce_fusion.3
  11.6 29.8 %reduce-scatter.3.cloned.1.call-done = bf16[64,2048]{1,0:T(8,128)(2,1)} async-done(((bf16[256,2048]{1,0:T(8,128)(2,1)}), bf16[64,2048]{1,0:T(8,128)(2,1)}) %reduce-scatter.3.cloned.1.call-update) | async-done | bytes 262160 | tf_op jit(solution)/shard_map/reduce_scatter | solution.py:46
  41.4 1.1 fusion.27
  42.5 1.1 fusion.29
  43.6 0.8 convolution_convert_fusion
  44.4 1.1 broadcast_in_dim.80
  45.5 189.4 %all_to_all.10 = bf16[32,8,8,2048]{3,2,1,0:T(8,128)(2,1)} all-to-all(bf16[32,8,8,2048]{3,2,1,0:T(8,128)(2,1)S(1)} %bitcast.88), channel_id=1, replica_groups=mesh['dp'=4,'ep'=8] {'dp','ep'}, dimensions={0} | all-to-all | bytes 16777216 | tf_op jit(solution)/shard_map/all_to_all | solution.py:84
  234.9 14.1 %fusion.4 = f32[8,32,8,352]{3,2,1,0:T(8,128)} fusion(bf16[8,2048,352]{1,2,0:T(8,128)(2,1)} %param.22, bf16[32,8,8,2048]{3,2,1,0:T(8,128)(2,1)} %all_to_all.10), kind=kOutput, calls=%fused_computation.4 | convolution fusion | flops 2952790016 | bytes 22806528 | tf_op jit(solution)/shard_map/semd,edf->semf/dot_general | solution.py:20
  249.0 23.5 %convert_bitcast_fusion = bf16[32,8,8,2048]{3,2,0,1:T(8,128)(2,1)} fusion(bf16[8,352,2048]{2,1,0:T(8,128)(2,1)} %param.24, f32[8,32,8,352]{3,2,1,0:T(8,128)} %fusion.4, bf16[8,2048,352]{1,2,0:T(8,128)(2,1)} %param.23, bf16[32,8,8,2048]{3,2,1,0:T(8,128)(2,1)} %all_to_all.10), kind=kOutput, calls=%fused_computation.6 | convolution fusion | flops 5914099712 | bytes 42729472 | tf_op jit(solution)/shard_map/semf,efd->semd/dot_general | solution.py:23
  272.5 8.3 %copy.34 = bf16[32,8,8,2048]{3,2,1,0:T(8,128)(2,1)} copy(bf16[32,8,8,2048]{3,2,0,1:T(8,128)(2,1)} %convert_bitcast_fusion) | data formatting | bytes 16777216 | tf_op jit(solution)/shard_map/convert_element_type | solution.py:88
  280.7 3.7 all-to-all-start.1
  284.5 0.7 all-gather.2.cloned.1.call-update
  285.2 0.2 reduce-scatter.5.cloned.1.call-start
  285.4 52.7 %all-gather.2.cloned.1.call-done = bf16[512,2048]{1,0:T(8,128)(2,1)} async-done(((bf16[64,2048]{1,0:T(8,128)(2,1)}), bf16[512,2048]{1,0:T(8,128)(2,1)}) %all-gather.2.cloned.1.call-update) | async-done | bytes 2097168 | tf_op jit(solution)/shard_map/all_gather | solution.py:99
  338.1 5.2 %fusion.43 = f32[512,704]{0,1:T(8,128)} fusion(bf16[512,2048]{1,0:T(8,128)(2,1)} %all-gather.2.cloned.1.call-done, bf16[2048,704]{0,1:T(8,128)(2,1)} %param.25), kind=kOutput, calls=%fused_computation.61 | convolution fusion | flops 1476395008 | bytes 6422528 | tf_op jit(solution)/shard_map/dot_general | solution.py:100
  343.3 7.7 %convolution_convert_fusion.1 = bf16[512,2048]{1,0:T(8,128)(2,1)} fusion(bf16[704,2048]{1,0:T(8,128)(2,1)S(1)} %copy-done, bf16[512,2048]{1,0:T(8,128)(2,1)} %all-gather.2.cloned.1.call-done, bf16[2048,704]{0,1:T(8,128)(2,1)} %param.26, f32[512,704]{0,1:T(8,128)} %fusion.43), kind=kOutput, calls=%fused_computation.17 | convolution fusion | flops 2956001280 | bytes 11403264 | tf_op jit(solution)/shard_map/dot_general | solution.py:105
  351.1 1.2 fusion.44
  352.4 0.1 select_reduce_fusion
  352.6 0.2 fusion.23
  352.7 153.1 %all-to-all-done.1 = bf16[32,8,8,2048]{3,2,1,0:T(8,128)(2,1)} async-done(((bf16[32,8,8,2048]{3,2,1,0:T(8,128)(2,1)}), bf16[32,8,8,2048]{3,2,1,0:T(8,128)(2,1)}, u32[]{:S(2)}, u32[]{:S(2)}) %all-to-all-start.1) | async-done | bytes 8388640 | tf_op jit(solution)/shard_map/all_to_all | solution.py:89
  505.8 7.3 %reduce_sum.81 = bf16[8,8,8,2048]{3,2,1,0:T(8,128)(2,1)} reduce(bf16[4,8,8,8,2048]{4,3,2,1,0:T(8,128)(2,1)} %bitcast.15, bf16[]{:T(256)} %constant.24.clone.1), dimensions={0}, to_apply=%region_11.12 | reduce | flops 3145728 | bytes 10485762 | tf_op jit(solution)/shard_map/reduce_sum | solution.py:92
  513.1 2.2 fusion.24
  515.4 0.8 fusion.32
  (43 shorter events, 0.9 us)
Async XLA Ops:
  7.2 336.2 %copy-start = (bf16[704,2048]{1,0:T(8,128)(2,1)S(1)}, bf16[704,2048]{1,0:T(8,128)(2,1)}, u32[]{:S(2)}) copy-start(bf16[704,2048]{1,0:T(8,128)(2,1)} %param.27) | copy-start | bytes 8650756
  7.2 3.6 copy-start.6
  7.2 4.1 copy-start.7
  7.2 4.1 copy-start.10
  7.2 34.2 %copy-start.3 = (bf16[1,64,2048]{2,1,0:T(8,128)(2,1)S(1)}, bf16[1,64,2048]{2,1,0:T(8,128)(2,1)}, u32[]{:S(2)}) copy-start(bf16[1,64,2048]{2,1,0:T(8,128)(2,1)} %param.16) | copy-start | bytes 786436
  7.2 34.2 %reduce-scatter.3.cloned.1.call-start = ((), (), s32[]{:S(2)}) async-start(), calls=%async_computation.4 | async-start | bytes 1310720 | tf_op jit(solution)/shard_map/reduce_scatter | solution.py:46
  43.6 1.9 copy-start.1
  280.7 225.1 %all-to-all-start.1 = ((bf16[32,8,8,2048]{3,2,1,0:T(8,128)(2,1)}), bf16[32,8,8,2048]{3,2,1,0:T(8,128)(2,1)}, u32[]{:S(2)}, u32[]{:S(2)}) async-start(bf16[32,8,8,2048]{3,2,1,0:T(8,128)(2,1)} %copy.34), calls=%async_computation.3 | async-start | bytes 16777216 | tf_op jit(solution)/shard_map/all_to_all | solution.py:89
  284.4 53.7 %all-gather.2.cloned.1.call-start = ((), (), s32[]{:S(2)}) async-start(), calls=%async_computation.5 | async-start | bytes 2359296 | tf_op jit(solution)/shard_map/all_gather | solution.py:99
  285.2 227.9 %reduce-scatter.5.cloned.1.call-start = ((), (), s32[]{:S(2)}) async-start(), calls=%async_computation.6 | async-start | bytes 2359296 | tf_op jit(solution)/shard_map/reduce_scatter | solution.py:104
  343.3 7.7 %copy-start.8 = (bf16[2048]{0:T(1024)(128)(2,1)S(1)}, bf16[2048]{0:T(1024)(128)(2,1)}, u32[]{:S(2)}) copy-start(bf16[2048]{0:T(1024)(128)(2,1)} %param.28) | copy-start | bytes 12292
  343.3 7.8 %copy-start.9 = (bf16[2048]{0:T(1024)(128)(2,1)S(1)}, bf16[2048]{0:T(1024)(128)(2,1)}, u32[]{:S(2)}) copy-start(bf16[2048]{0:T(1024)(128)(2,1)} %param.29) | copy-start | bytes 12292
  343.3 7.8 %copy-start.2 = (bf16[64,2048]{1,0:T(8,128)(2,1)S(1)}, bf16[64,2048]{1,0:T(8,128)(2,1)}, u32[]{:S(2)}) copy-start(bf16[64,2048]{1,0:T(8,128)(2,1)} %copy-done.1) | copy-start | bytes 786436
  505.8 7.3 %copy-start.4 = (bf16[64,2048]{1,0:T(8,128)(2,1)S(1)}, bf16[64,2048]{1,0:T(8,128)(2,1)}, u32[]{:S(2)}) copy-start(bf16[64,2048]{1,0:T(8,128)(2,1)} %reduce-scatter.3.cloned.1.call-done) | copy-start | bytes 786436
  515.3 0.9 copy-start.5
Sparse Core Ops, SparseCore 0:
  10.9 30.4 reduce-scatter.2
  287.5 50.5 all-gather.1
  351.2 73.7 reduce-scatter.4
where the time goes:
time: 523 us
  waiting for transfers between devices  236 us (45%)
  blocking collectives  189 us (36%)
  matrix products  58.4 us (11%)
  between operations  14 us (3%)
  other arithmetic  11.1 us (2%)
  local copies, waits for them, and re-layouts  9.59 us (2%)
    all_to_all x1, blocking collectives, per_device(): lax.all_to_all(copies, ('dp', 'ep'), split_axis=0, concat_axis=0, tiled=T...  189 us
    all_to_all x1, waiting for transfers between devices, per_device(): lax.all_to_all(partial_value, ('dp', 'ep'), split_axis=0, concat_axis=0,...  153 us
    all_gather x1, waiting for transfers between devices, per_device(): row_block = lax.all_gather(normed, 'ep', axis=0, tiled=True)  52.7 us
    reduce_scatter x1, waiting for transfers between devices, per_device(): lax.psum_scatter(jnp.dot(row_block, w_out, preferred_element_type=jnp.flo...  29.8 us
    dot_general x1, matrix products, expert_partial(): jnp.einsum('semf,efd->semd', hidden, w_down, preferred_element_type=jnp.f...  23.5 us
    dot_general x1, matrix products, expert_partial(): jnp.einsum('semd,edf->semf', rows_in, w_gate, preferred_element_type=jnp....  14.1 us
  transfers between devices with their start and end apart: 4, of which 3 were waited for; matrix products, arithmetic and copies ran while one was open for 4% of the time, Pallas kernels for 0%

commit v1 on v0

--- a/solution.py
+++ b/solution.py
@@ -1,3 +1,4 @@
+import functools
 import jax
 import jax.numpy as jnp
 from jax import lax
@@ -5,6 +6,21 @@
 
 MOST = 8
 eps_norm = 1e-06
+
+
+def map_group(content, k_dim):
+    axis_len = lax.axis_size("ep")
+    samples = [(d, (d + 1) % axis_len) for d in range(axis_len)]
+    current_block = [None] * axis_len
+    current_block[axis_len - 1] = content
+    for ix in range(axis_len - 2, -1, -1):
+        current_block[ix] = lax.ppermute(current_block[ix + 1], "ep", samples)
+    t1 = jnp.concatenate(current_block, k_dim)
+    passed = (lax.axis_index("ep") + 1) * content.shape[k_dim]
+    return jnp.roll(t1, passed, k_dim)
+
+
+vector_start = functools.partial(map_group, k_dim=0)
 
 
 def rms_scale(values_in, gain_vec):
@@ -96,7 +112,7 @@
     routed = jnp.dot(
         combine_mat, returned.reshape(buffer_cells, model_width), preferred_element_type=jnp.float32
     )
-    row_block = lax.all_gather(normed, "ep", axis=0, tiled=True)
+    row_block = vector_start(normed)
     gate_part = jnp.dot(row_block, w_shared_gate, preferred_element_type=jnp.float32)
     up_part = jnp.dot(row_block, w_shared_up, preferred_element_type=jnp.float32)
     hidden_all = (jax.nn.silu(gate_part) * up_part).astype(jnp.bfloat16)

time: 523 us -> 575 us (1.099)
  starting transfers between devices: 3.97 us -> 42.2 us
  local copies, waits for them, and re-layouts: 9.59 us -> 23.9 us
    ppermute x0 -> x7, waiting for transfers between devices: none -> 175 us  [map_group(): current_block[ix] = lax.ppermute(current_block[ix + 1], 'ep', samples)]
    all_to_all x1, waiting for transfers between devices: 153 us -> 0.01 us  [per_device(): lax.all_to_all(partial_value, ('dp', 'ep'), split_axis=0, concat_axis=0,...]
    all_gather x1 -> x0, waiting for transfers between devices: 52.7 us -> none  [per_device(): row_block = lax.all_gather(normed, 'ep', axis=0, tiled=True)]
    ppermute x0 -> x7, starting transfers between devices: none -> 38.4 us  [map_group(): current_block[ix] = lax.ppermute(current_block[ix + 1], 'ep', samples)]
    reduce_scatter x1, waiting for transfers between devices: 0.01 us -> 32.5 us  [per_device(): lax.psum_scatter(jnp.dot(row_block, w_shared_down, preferred_element_type...]
    unnamed x23 -> x58, local copies, waits for them, and re-layouts: 0.06 us -> 14.3 us
  transfers between devices with their start and end apart: 4 -> 10, of which waited for: 3 -> 9; matrix products, arithmetic and copies ran while one was open for 4% -> 5% of each run, Pallas kernels for 0% -> 0%
where the time goes in v1:
time: 575 us
  waiting for transfers between devices  238 us (41%)
  blocking collectives  189 us (33%)
  matrix products  56 us (10%)
  starting transfers between devices  42.2 us (7%)
  local copies, waits for them, and re-layouts  23.9 us (4%)
  between operations  14.4 us (3%)
  other arithmetic  11.1 us (2%)
    all_to_all x1, blocking collectives, per_device(): lax.all_to_all(copies, ('dp', 'ep'), split_axis=0, concat_axis=0, tiled=T...  189 us
    ppermute x7, waiting for transfers between devices, map_group(): current_block[ix] = lax.ppermute(current_block[ix + 1], 'ep', samples)  175 us
    ppermute x7, starting transfers between devices, map_group(): current_block[ix] = lax.ppermute(current_block[ix + 1], 'ep', samples)  38.4 us
    reduce_scatter x1, waiting for transfers between devices, per_device(): lax.psum_scatter(jnp.dot(row_block, w_shared_down, preferred_element_type...  32.5 us
    reduce_scatter x1, waiting for transfers between devices, per_device(): lax.psum_scatter(jnp.dot(row_block, w_out, preferred_element_type=jnp.flo...  29.8 us
    dot_general x1, matrix products, expert_partial(): jnp.einsum('semf,efd->semd', hidden, w_down, preferred_element_type=jnp.f...  23.5 us
    unnamed x58, local copies, waits for them, and re-layouts  14.3 us
    dot_general x1, matrix products, expert_partial(): jnp.einsum('semd,edf->semf', rows_in, w_gate, preferred_element_type=jnp....  14.1 us
  transfers between devices with their start and end apart: 10, of which 9 were waited for; matrix products, arithmetic and copies ran while one was open for 5% of the time, Pallas kernels for 0%

profile of v1, /device:TPU:0, one launch (start us, length us, event | category | flops | bytes accessed | tf_op | source)
XLA Modules:
  0.0 574.8 jit_solution(17200336297412271853)
XLA Ops:
  7.3 3.5 convolution_convert_fusion.2
  11.6 29.8 %reduce-scatter.3.cloned.1.call-done = bf16[64,2048]{1,0:T(8,128)(2,1)} async-done(((bf16[256,2048]{1,0:T(8,128)(2,1)}), bf16[64,2048]{1,0:T(8,128)(2,1)}) %reduce-scatter.3.cloned.1.call-update) | async-done | bytes 262160 | tf_op jit(solution)/shard_map/reduce_scatter | solution.py:62
  45.5 189.4 %all_to_all.10 = bf16[32,8,8,2048]{3,2,1,0:T(8,128)(2,1)} all-to-all(bf16[32,8,8,2048]{3,2,1,0:T(8,128)(2,1)S(1)} %bitcast.86), channel_id=1, replica_groups=mesh['dp'=4,'ep'=8] {'dp','ep'}, dimensions={0} | all-to-all | bytes 16777216 | tf_op jit(solution)/shard_map/all_to_all | solution.py:100
  234.9 14.1 %fusion.4 = f32[8,32,8,352]{3,2,1,0:T(8,128)} fusion(bf16[8,2048,352]{1,2,0:T(8,128)(2,1)} %param.22, bf16[32,8,8,2048]{3,2,1,0:T(8,128)(2,1)} %all_to_all.10), kind=kOutput, calls=%fused_computation.4 | convolution fusion | flops 2952790016 | bytes 22806528 | tf_op jit(solution)/shard_map/semd,edf->semf/dot_general | solution.py:36
  249.0 23.5 %convert_bitcast_fusion = bf16[32,8,8,2048]{3,2,0,1:T(8,128)(2,1)} fusion(bf16[8,352,2048]{2,1,0:T(8,128)(2,1)} %param.24, f32[8,32,8,352]{3,2,1,0:T(8,128)} %fusion.4, bf16[8,2048,352]{1,2,0:T(8,128)(2,1)} %param.23, bf16[32,8,8,2048]{3,2,1,0:T(8,128)(2,1)} %all_to_all.10), kind=kOutput, calls=%fused_computation.6 | convolution fusion | flops 5914099712 | bytes 42729472 | tf_op jit(solution)/shard_map/semf,efd->semd/dot_general | solution.py:39
  272.5 8.3 %copy.34 = bf16[32,8,8,2048]{3,2,1,0:T(8,128)(2,1)} copy(bf16[32,8,8,2048]{3,2,0,1:T(8,128)(2,1)} %convert_bitcast_fusion) | data formatting | bytes 16777216 | tf_op jit(solution)/shard_map/convert_element_type | solution.py:104
  280.7 3.7 all-to-all-start.1
  284.5 143.2 %collective-permute-done = bf16[64,2048]{1,0:T(8,128)(2,1)S(1)} collective-permute-done((bf16[64,2048]{1,0:T(8,128)(2,1)S(1)}, bf16[64,2048]{1,0:T(8,128)(2,1)S(1)}, u32[]{:S(2)}, u32[]{:S(2)}) %collective-permute-start) | collective-permute-done | bytes 262176 | tf_op jit(solution)/shard_map/ppermute | solution.py:17
  428.4 7.7 %collective-permute-done.1 = bf16[64,2048]{1,0:T(8,128)(2,1)S(1)} collective-permute-done((bf16[64,2048]{1,0:T(8,128)(2,1)S(1)}, bf16[64,2048]{1,0:T(8,128)(2,1)S(1)}, u32[]{:S(2)}, u32[]{:S(2)}) %collective-permute-start.1) | collective-permute-done | bytes 262176 | tf_op jit(solution)/shard_map/ppermute | solution.py:17
  436.8 7.7 %collective-permute-done.2 = bf16[64,2048]{1,0:T(8,128)(2,1)S(1)} collective-permute-done((bf16[64,2048]{1,0:T(8,128)(2,1)S(1)}, bf16[64,2048]{1,0:T(8,128)(2,1)S(1)}, u32[]{:S(2)}, u32[]{:S(2)}) %collective-permute-start.2) | collective-permute-done | bytes 262176 | tf_op jit(solution)/shard_map/ppermute | solution.py:17
  445.2 30.5 %collective-permute-start.3 = (bf16[64,2048]{1,0:T(8,128)(2,1)S(1)}, bf16[64,2048]{1,0:T(8,128)(2,1)S(1)}, u32[]{:S(2)}, u32[]{:S(2)}) collective-permute-start(bf16[64,2048]{1,0:T(8,128)(2,1)S(1)} %collective-permute-done.2), channel_id=1, source_target_pairs={{0,1},{1,2},{2,3},{3,4},{4,5},{5,6},{6,7},{7,0},{8,9},{9,10},{10,1... | collective-permute-start | bytes 786440 | tf_op jit(solution)/shard_map/ppermute | solution.py:17
  475.8 1.2 collective-permute-done.3
  477.6 4.6 collective-permute-start.4
  482.3 3.3 collective-permute-done.4
  486.2 2.5 collective-permute-start.5
  488.8 5.2 collective-permute-done.5
  494.6 7.2 %collective-permute-done.6 = bf16[64,2048]{1,0:T(8,128)(2,1)} collective-permute-done((bf16[64,2048]{1,0:T(8,128)(2,1)}, bf16[64,2048]{1,0:T(8,128)(2,1)}, u32[]{:S(2)}, u32[]{:S(2)}) %collective-permute-start.6) | collective-permute-done | bytes 262176 | tf_op jit(solution)/shard_map/ppermute | solution.py:17
  510.9 1.9 copy-done.15
  512.8 2.8 fusion.19
  515.6 7.7 %convolution_convert_fusion.1 = bf16[512,2048]{1,0:T(8,128)(2,1)} fusion(bf16[704,2048]{1,0:T(8,128)(2,1)S(1)} %copy-done, f32[512,704]{0,1:T(8,128)} %fusion.19, bf16[2048,704]{0,1:T(8,128)(2,1)} %param.25, bf16[1024,2048]{1,0:T(8,128)(2,1)} %copy-done.15, s32[]{:T(128)S(6)} %select_n.30), kind=kOutput, calls=%fused_computation.17 | convolution fusion | flops 2956001280 | bytes 11403268 | tf_op jit(solution)/shard_map/dot_general | solution.py:121
  523.4 1.2 fusion.54
  525.0 7.3 %reduce_sum.81 = bf16[8,8,8,2048]{3,2,1,0:T(8,128)(2,1)} reduce(bf16[4,8,8,8,2048]{4,3,2,1,0:T(8,128)(2,1)} %bitcast.15, bf16[]{:T(256)} %constant.53.clone.1), dimensions={0}, to_apply=%region_11.12 | reduce | flops 3145728 | bytes 10485762 | tf_op jit(solution)/shard_map/reduce_sum | solution.py:108
  532.3 32.5 %reduce-scatter.5.cloned.1.call-done = bf16[64,2048]{1,0:T(8,128)(2,1)} async-done(((bf16[512,2048]{1,0:T(8,128)(2,1)}), bf16[64,2048]{1,0:T(8,128)(2,1)}) %reduce-scatter.5.cloned.1.call-update) | async-done | bytes 262160 | tf_op jit(solution)/shard_map/reduce_scatter | solution.py:120
  564.8 2.2 fusion.32
  (90 shorter events, 19.3 us)
Async XLA Ops:
  7.2 508.4 %copy-start = (bf16[704,2048]{1,0:T(8,128)(2,1)S(1)}, bf16[704,2048]{1,0:T(8,128)(2,1)}, u32[]{:S(2)}) copy-start(bf16[704,2048]{1,0:T(8,128)(2,1)} %param.27) | copy-start | bytes 8650756
  7.2 3.6 copy-start.16
  7.2 3.6 copy-start.14
  7.2 4.1 copy-start.19
  7.2 34.2 %copy-start.1 = (bf16[1,64,2048]{2,1,0:T(8,128)(2,1)S(1)}, bf16[1,64,2048]{2,1,0:T(8,128)(2,1)}, u32[]{:S(2)}) copy-start(bf16[1,64,2048]{2,1,0:T(8,128)(2,1)} %param.16) | copy-start | bytes 786436
  7.2 34.2 %reduce-scatter.3.cloned.1.call-start = ((), (), s32[]{:S(2)}) async-start(), calls=%async_computation.4 | async-start | bytes 1310720 | tf_op jit(solution)/shard_map/reduce_scatter | solution.py:62
  280.7 244.3 %all-to-all-start.1 = ((bf16[32,8,8,2048]{3,2,1,0:T(8,128)(2,1)}), bf16[32,8,8,2048]{3,2,1,0:T(8,128)(2,1)}, u32[]{:S(2)}, u32[]{:S(2)}) async-start(bf16[32,8,8,2048]{3,2,1,0:T(8,128)(2,1)} %copy.34), calls=%async_computation.3 | async-start | bytes 16777216 | tf_op jit(solution)/shard_map/all_to_all | solution.py:105
  284.4 280.4 %reduce-scatter.5.cloned.1.call-start = ((), (), s32[]{:S(2)}) async-start(), calls=%async_computation.5 | async-start | bytes 2359296 | tf_op jit(solution)/shard_map/reduce_scatter | solution.py:120
  284.5 143.3 %collective-permute-start = (bf16[64,2048]{1,0:T(8,128)(2,1)S(1)}, bf16[64,2048]{1,0:T(8,128)(2,1)S(1)}, u32[]{:S(2)}, u32[]{:S(2)}) collective-permute-start(bf16[64,2048]{1,0:T(8,128)(2,1)S(1)} %fusion.37), channel_id=1, source_target_pairs={{0,1},{1,2},{2,3},{3,4},{4,5},{5,6},{6,7},{7,0},{8,9},{9,10},{10,1... | collective-permute-start | bytes 786440 | tf_op jit(solution)/shard_map/ppermute | solution.py:17
  428.4 7.7 %collective-permute-start.1 = (bf16[64,2048]{1,0:T(8,128)(2,1)S(1)}, bf16[64,2048]{1,0:T(8,128)(2,1)S(1)}, u32[]{:S(2)}, u32[]{:S(2)}) collective-permute-start(bf16[64,2048]{1,0:T(8,128)(2,1)S(1)} %collective-permute-done), channel_id=1, source_target_pairs={{0,1},{1,2},{2,3},{3,4},{4,5},{5,6},{6,7},{7,0},{8,9},{9,10},{10,1... | collective-permute-start | bytes 786440 | tf_op jit(solution)/shard_map/ppermute | solution.py:17
  436.8 7.7 %collective-permute-start.2 = (bf16[64,2048]{1,0:T(8,128)(2,1)S(1)}, bf16[64,2048]{1,0:T(8,128)(2,1)S(1)}, u32[]{:S(2)}, u32[]{:S(2)}) collective-permute-start(bf16[64,2048]{1,0:T(8,128)(2,1)S(1)} %collective-permute-done.1), channel_id=1, source_target_pairs={{0,1},{1,2},{2,3},{3,4},{4,5},{5,6},{6,7},{7,0},{8,9},{9,10},{10,1... | collective-permute-start | bytes 786440 | tf_op jit(solution)/shard_map/ppermute | solution.py:17
  445.2 31.7 %collective-permute-start.3 = (bf16[64,2048]{1,0:T(8,128)(2,1)S(1)}, bf16[64,2048]{1,0:T(8,128)(2,1)S(1)}, u32[]{:S(2)}, u32[]{:S(2)}) collective-permute-start(bf16[64,2048]{1,0:T(8,128)(2,1)S(1)} %collective-permute-done.2), channel_id=1, source_target_pairs={{0,1},{1,2},{2,3},{3,4},{4,5},{5,6},{6,7},{7,0},{8,9},{9,10},{10,1... | collective-permute-start | bytes 786440 | tf_op jit(solution)/shard_map/ppermute | solution.py:17
  477.6 7.9 %collective-permute-start.4 = (bf16[64,2048]{1,0:T(8,128)(2,1)S(1)}, bf16[64,2048]{1,0:T(8,128)(2,1)S(1)}, u32[]{:S(2)}, u32[]{:S(2)}) collective-permute-start(bf16[64,2048]{1,0:T(8,128)(2,1)S(1)} %collective-permute-done.3), channel_id=1, source_target_pairs={{0,1},{1,2},{2,3},{3,4},{4,5},{5,6},{6,7},{7,0},{8,9},{9,10},{10,1... | collective-permute-start | bytes 786440 | tf_op jit(solution)/shard_map/ppermute | solution.py:17
  486.2 7.7 %collective-permute-start.5 = (bf16[64,2048]{1,0:T(8,128)(2,1)S(1)}, bf16[64,2048]{1,0:T(8,128)(2,1)}, u32[]{:S(2)}, u32[]{:S(2)}) collective-permute-start(bf16[64,2048]{1,0:T(8,128)(2,1)S(1)} %collective-permute-done.4), channel_id=1, source_target_pairs={{0,1},{1,2},{2,3},{3,4},{4,5},{5,6},{6,7},{7,0},{8,9},{9,10},{10,1... | collective-permute-start | bytes 786440 | tf_op jit(solution)/shard_map/ppermute | solution.py:17
  493.9 7.9 %collective-permute-start.6 = (bf16[64,2048]{1,0:T(8,128)(2,1)}, bf16[64,2048]{1,0:T(8,128)(2,1)}, u32[]{:S(2)}, u32[]{:S(2)}) collective-permute-start(bf16[64,2048]{1,0:T(8,128)(2,1)} %collective-permute-done.5), channel_id=1, source_target_pairs={{0,1},{1,2},{2,3},{3,4},{4,5},{5,6},{6,7},{7,0},{8,9},{9,10},{10,1... | collective-permute-start | bytes 786440 | tf_op jit(solution)/shard_map/ppermute | solution.py:17
  494.6 16.1 %copy-start.13 = (bf16[64,2048]{1,0:T(8,128)(2,1)S(1)}, bf16[64,2048]{1,0:T(8,128)(2,1)}, u32[]{:S(2)}) copy-start(bf16[64,2048]{1,0:T(8,128)(2,1)} %copy-done.12) | copy-start | bytes 786436
  494.6 16.1 %copy-start.11 = (bf16[64,2048]{1,0:T(8,128)(2,1)S(1)}, bf16[64,2048]{1,0:T(8,128)(2,1)}, u32[]{:S(2)}) copy-start(bf16[64,2048]{1,0:T(8,128)(2,1)} %copy-done.10) | copy-start | bytes 786436
  494.6 16.1 %copy-start.9 = (bf16[64,2048]{1,0:T(8,128)(2,1)S(1)}, bf16[64,2048]{1,0:T(8,128)(2,1)}, u32[]{:S(2)}) copy-start(bf16[64,2048]{1,0:T(8,128)(2,1)} %copy-done.8) | copy-start | bytes 786436
  494.6 16.2 %copy-start.7 = (bf16[64,2048]{1,0:T(8,128)(2,1)S(1)}, bf16[64,2048]{1,0:T(8,128)(2,1)}, u32[]{:S(2)}) copy-start(bf16[64,2048]{1,0:T(8,128)(2,1)} %copy-done.6) | copy-start | bytes 786436
  494.6 16.2 %copy-start.5 = (bf16[64,2048]{1,0:T(8,128)(2,1)S(1)}, bf16[64,2048]{1,0:T(8,128)(2,1)}, u32[]{:S(2)}) copy-start(bf16[64,2048]{1,0:T(8,128)(2,1)} %copy-done.4) | copy-start | bytes 786436
  494.6 18.2 %copy-start.20 = (bf16[2048,704]{0,1:T(8,128)(2,1)S(1)}, bf16[2048,704]{0,1:T(8,128)(2,1)}, u32[]{:S(2)}) copy-start(bf16[2048,704]{0,1:T(8,128)(2,1)} %param.26) | copy-start | bytes 8650756
  515.6 7.8 %copy-start.17 = (bf16[2048]{0:T(1024)(128)(2,1)S(1)}, bf16[2048]{0:T(1024)(128)(2,1)}, u32[]{:S(2)}) copy-start(bf16[2048]{0:T(1024)(128)(2,1)} %param.28) | copy-start | bytes 12292
  515.6 7.8 %copy-start.18 = (bf16[2048]{0:T(1024)(128)(2,1)S(1)}, bf16[2048]{0:T(1024)(128)(2,1)}, u32[]{:S(2)}) copy-start(bf16[2048]{0:T(1024)(128)(2,1)} %param.29) | copy-start | bytes 12292
  525.0 39.8 %copy-start.2 = (bf16[64,2048]{1,0:T(8,128)(2,1)S(1)}, bf16[64,2048]{1,0:T(8,128)(2,1)}, u32[]{:S(2)}) copy-start(bf16[64,2048]{1,0:T(8,128)(2,1)} %reduce-scatter.3.cloned.1.call-done) | copy-start | bytes 786436
  (7 other events, 6.3 us)
Sparse Core Ops, SparseCore 0:
  10.9 30.4 reduce-scatter.2
  523.5 41.3 reduce-scatter.4
